TPU v7x, 32 devices: a whole 2x2x4 slice. The times are simulated.
32 devices in a mesh: inv: 2 (over y), depth: 4 (over z), shot: 2 (over x), lat: 2 (over core).
Axes of the slice: x: 2, y: 2, z: 4, core: 2. Of those that a mesh axis runs over, the one named last changes fastest.
Arguments:
- model_field: float32 [128, 64, 128], P(('inv', 'depth'), 'lat'), parts along dimension 0, may hold values from 0.02 to 0.08
- buoyancy: float32 [128, 64, 128], P(('inv', 'depth'), 'lat'), parts along dimension 0, may hold values from 0.5 to 1.5
- forward_pair: float32 [4, 2, 64, 64, 128], P(('inv', 'shot'), None, 'depth', 'lat'), parts along dimension 0, may hold values from -6 to 6
- adjoint_pair: float32 [4, 2, 64, 64, 128], P(('inv', 'shot'), None, 'depth', 'lat'), parts along dimension 0, may hold values from -6 to 6
- stored_states: bfloat16 [4, 6, 64, 64, 128], P(('inv', 'shot'), None, 'depth', 'lat'), parts along dimension 0, may hold values from -6 to 6
- momentum: float32 [128, 64, 128], P(('inv', 'depth', 'shot'), 'lat'), parts along dimension 0, may hold values from -4 to 4
- wavelet: float32 [8, 4], P('inv'), parts along dimension 0, may hold values from -6 to 6
- residuals: float32 [8, 4, 256], P('inv'), parts along dimension 0, may hold values from -6 to 6
- source_cells: int32 [8], P('inv'), parts along dimension 0, may hold values from 0 to 524287
- receiver_cells: int32 [8, 256], P('inv'), parts along dimension 0, may hold values from 0 to 524287
- assignment: int32 [8], P('inv'), parts along dimension 0, may hold values from 0 to 3, each once
Outputs:
- forward_out: float32 [4, 2, 64, 64, 128], P(('inv', 'shot'), None, 'depth', 'lat'), parts along dimension 0
- adjoint_out: float32 [4, 2, 64, 64, 128], P(('inv', 'shot'), None, 'depth', 'lat'), parts along dimension 0
- momentum_new: float32 [128, 64, 128], P(('inv', 'depth', 'shot'), 'lat'), parts along dimension 0
- model_new: float32 [128, 64, 128], P(('inv', 'depth', 'shot'), 'lat'), parts along dimension 0
There are 2 independent parts, one for each index of `inv`. A program takes and returns all parts, laid end to end along the dimension named above; each array names one. Nothing has to cross between parts.
Inputs may be any that keep to these rules, and one draw needn't show every extreme that they name: `source_cells`: flattened cell index of each shot's source. `receiver_cells`: flattened cell indices of each shot's receivers; cells may repeat. `assignment`: a permutation of the 4 shots.
All inputs are finite; a program needn't handle non-finite values.
Results may differ from a plain program's by a relative error of at most 0.0003.
Values sent between devices are 32-bit elements; how exact they have to be, the bound alone decides.
A program may use at most 64 MiB of HBM per device.

v0:
```python
import jax
import jax.numpy as jnp
from jax import lax
from jax.sharding import PartitionSpec as P

SECOND_TAPS = (8.0 / 5.0, -1.0 / 5.0, 8.0 / 315.0, -1.0 / 560.0)
CENTER_TAP = -205.0 / 72.0
FIRST_TAPS = (4.0 / 5.0, -1.0 / 5.0, 4.0 / 105.0, -1.0 / 280.0)
MOMENT_KEEP = 0.9
STEP_RATE = 0.02


def extended(cells, sides, width):
    for axis, dim in sides:
        count = lax.axis_size(axis)
        ends = count - 1
        head = lax.slice_in_dim(cells, 0, width, axis=dim)
        tail = lax.slice_in_dim(cells, cells.shape[dim] - width, cells.shape[dim], axis=dim)
        cells = jnp.concatenate(
            [
                lax.ppermute(tail, axis, [(i, (i + 1) % count) for i in range(ends)]),
                cells,
                lax.ppermute(head, axis, [((i + 1) % count, i) for i in range(ends)]),
            ],
            axis=dim,
        )
    return cells


def offset_core(padded, along_axis, offset):
    pieces = [slice(None)] * (padded.ndim - 3)
    for axis_id in range(2):
        length = padded.shape[padded.ndim - 3 + axis_id] - 8
        begin = 4 + (offset if axis_id == along_axis else 0)
        pieces.append(slice(begin, begin + length))
    pieces.append(slice(None))
    core = padded[tuple(pieces)]
    if along_axis != 2 or offset == 0:
        return core
    columns = core.shape[-1]
    rolled = jnp.roll(core, -offset, axis=core.ndim - 1)
    column_ids = jnp.arange(columns, dtype=jnp.int32) + offset
    valid = (column_ids >= 0) & (column_ids < columns)
    return jnp.where(valid, rolled, 0.0)


def second_sum(padded):
    total = 3.0 * CENTER_TAP * offset_core(padded, 0, 0)
    for axis_id in range(3):
        for reach in range(1, 5):
            total = total + SECOND_TAPS[reach - 1] * (
                offset_core(padded, axis_id, reach) + offset_core(padded, axis_id, -reach)
            )
    return total


def first_diff(padded, axis_id):
    total = FIRST_TAPS[0] * (offset_core(padded, axis_id, 1) - offset_core(padded, axis_id, -1))
    for reach in range(2, 5):
        total = total + FIRST_TAPS[reach - 1] * (
            offset_core(padded, axis_id, reach) - offset_core(padded, axis_id, -reach)
        )
    return total


def operator(padded, buoy_core, slopes):
    result = buoy_core * second_sum(padded)
    for axis_id in range(3):
        result = result + slopes[axis_id] * first_diff(padded, axis_id)
    return result


def trim(array, cut):
    if cut == 0:
        return array
    lead = [slice(None)] * (array.ndim - 3)
    pieces = lead + [
        slice(cut, array.shape[-3] - cut),
        slice(cut, array.shape[-2] - cut),
        slice(None),
    ]
    return array[tuple(pieces)]


def place_values(field, cell_ids, amounts, depth_anchor, lateral_anchor, rows_all):
    columns = field.shape[2]
    depth_index = cell_ids // (rows_all * columns) - depth_anchor
    row_index = cell_ids // columns % rows_all - lateral_anchor
    column_index = cell_ids % columns
    inside = (
        (depth_index >= 0)
        & (depth_index < field.shape[0])
        & (row_index >= 0)
        & (row_index < field.shape[1])
    )
    depth_safe = jnp.clip(depth_index, 0, field.shape[0] - 1)
    row_safe = jnp.clip(row_index, 0, field.shape[1] - 1)
    return field.at[depth_safe, row_safe, column_index].add(jnp.where(inside, amounts, 0.0))


def local(
    model_field,
    buoyancy,
    forward_pair,
    adjoint_pair,
    stored_states,
    momentum,
    wavelet,
    residuals,
    source_cells,
    receiver_cells,
    assignment,
):
    depth_rank = lax.axis_index("depth")
    lat_rank = lax.axis_index("lat")
    shot_rank = lax.axis_index("shot")
    groups = lax.axis_size("shot")
    planes = model_field.shape[0]
    rows_dev = model_field.shape[1]
    rows_all = rows_dev * lax.axis_size("lat")
    steps_count = stored_states.shape[1] - 2
    fwd_shot = assignment[shot_rank]
    adj_shot = assignment[groups + shot_rank]
    source_cell = source_cells[fwd_shot][None]
    source_wave = wavelet[fwd_shot]
    receivers = receiver_cells[adj_shot]
    traces = residuals[adj_shot]
    previous = jnp.stack([forward_pair[0, 0], adjoint_pair[0, 0]])
    current = jnp.stack([forward_pair[0, 1], adjoint_pair[0, 1]])
    buoy_ext = extended(buoyancy, (("depth", 0), ("lat", 1)), 4)
    model_width = 0
    buoy_width = 4
    previous_width = 0
    slopes_full = tuple((first_diff(buoy_ext, axis_id) for axis_id in range(3)))
    imaging = jnp.zeros(model_field.shape, jnp.float32)
    for step in range(steps_count):
        current_ext = extended(current, (("depth", 1), ("lat", 2)), 4)
        width = 4
        out_width = width - 4
        states = stored_states[0, step : step + 3].astype(jnp.float32)
        imaging = imaging + trim(current_ext[1], width) * (states[2] - 2.0 * states[1] + states[0])
        buoy_core = trim(buoy_ext, buoy_width - out_width)
        slopes = tuple((trim(slope_part, buoy_width - 4 - out_width) for slope_part in slopes_full))
        model_core = trim(model_field, model_width - out_width)
        prev_core = trim(previous, previous_width - out_width)
        stepped = (
            2.0 * trim(current_ext, 4)
            - prev_core
            + model_core * operator(current_ext, buoy_core, slopes)
        )
        depth_anchor = depth_rank * planes - out_width
        lateral_anchor = lat_rank * rows_dev - out_width
        fwd_next = place_values(
            stepped[0], source_cell, source_wave[step][None], depth_anchor, lateral_anchor, rows_all
        )
        adj_next = place_values(
            stepped[1], receivers, traces[step], depth_anchor, lateral_anchor, rows_all
        )
        previous = trim(current_ext, 4)
        previous_width = out_width
        current = jnp.stack([fwd_next, adj_next])
    factor = 1.0 / (groups * steps_count)
    contribution = imaging * factor
    quarter = planes // groups
    share = lax.psum_scatter(contribution, "shot", scatter_dimension=0, tiled=True)
    own_model = lax.dynamic_slice_in_dim(model_field, shot_rank * quarter, quarter, 0)
    momentum_new = MOMENT_KEEP * momentum + share
    model_new = own_model - STEP_RATE * momentum_new
    forward_out = jnp.stack([previous[0], current[0]])[None]
    adjoint_out = jnp.stack([previous[1], current[1]])[None]
    return (forward_out, adjoint_out, momentum_new, model_new)


def solution(mesh):
    in_specs = (
        P(("inv", "depth"), "lat", None),
        P(("inv", "depth"), "lat", None),
        P(("inv", "shot"), None, "depth", "lat", None),
        P(("inv", "shot"), None, "depth", "lat", None),
        P(("inv", "shot"), None, "depth", "lat", None),
        P(("inv", "depth", "shot"), "lat", None),
        P("inv", None),
        P("inv", None, None),
        P("inv"),
        P("inv", None),
        P("inv"),
    )
    out_specs = (
        P(("inv", "shot"), None, "depth", "lat", None),
        P(("inv", "shot"), None, "depth", "lat", None),
        P(("inv", "depth", "shot"), "lat", None),
        P(("inv", "depth", "shot"), "lat", None),
    )
    return jax.shard_map(local, mesh=mesh, in_specs=in_specs, out_specs=out_specs, check_vma=False)
```

profile of v0, /device:TPU:0, one launch (start us, length us, event | category | flops | bytes accessed | tf_op | source)
XLA Modules:
  0.0 238.2 jit_solution(15935729598668112332)
XLA Ops:
  7.2 1.5 fusion.137
  8.8 1.3 collective-permute-start.4
  10.0 6.2 %collective-permute-start.5 = (f32[4,32,128]{2,1,0:T(8,128)}, f32[4,32,128]{2,1,0:T(8,128)}, u32[]{:S(2)}, u32[]{:S(2)}) collective-permute-start(f32[4,32,128]{2,1,0:T(8,128)} %get-tuple-element.176), channel_id=1, source_target_pairs={{0,4},{4,8},{8,12},{1,5},{5,9},{9,13},{2,6},{6,10},{10,14},{3,7},{... | collective-permute-start | bytes 196616 | tf_op jit(solution)/shard_map/ppermute | solution.py:21
  16.3 1.3 slice_bitcast_fusion.6
  18.2 3.3 %collective-permute-start.1 = (f32[2,4,32,128]{3,2,1,0:T(8,128)}, f32[2,4,32,128]{3,2,1,0:T(8,128)S(1)}, u32[]{:S(2)}, u32[]{:S(2)}) collective-permute-start(f32[2,4,32,128]{3,2,1,0:T(8,128)} %get-tuple-element.148), channel_id=1, source_target_pairs={{0,4},{4,8},{8,12},{1,5},{5,9},{9,13},{2,6},{6,10},{10,14},{3,7},{... | collective-permute-start | bytes 393224 | tf_op jit(solution)/shard_map/ppermute | solution.py:21
  21.5 1.3 collective-permute-start
  32.2 0.9 fusion.145
  33.1 0.9 fusion.144
  34.0 0.9 fusion.141
  34.9 0.9 fusion.143
  35.7 0.9 fusion.142
  36.7 0.9 fusion.139
  37.5 0.9 fusion.138
  38.4 1.1 fusion.57
  39.5 1.1 fusion.52
  40.6 1.1 fusion.53
  41.7 1.1 fusion.60
  42.9 1.2 fusion.61
  44.1 1.2 fusion.56
  45.2 1.1 fusion.49
  46.4 1.1 fusion.48
  50.6 1.8 slice_convert_fusion.3
  56.4 2.7 %fusion.114 = f32[16,32,128]{2,1,0:T(8,128)S(1)} fusion(f32[16,32,1]{2,1,0:T(8,128)} %get-tuple-element.190, f32[16,32,127]{2,1,0:T(8,128)} %get-tuple-element.192, f32[16,32,127]{2,1,0:T(8,128)} %get-tuple-element.191, f32[16,32,1]{2,1,0:T(8,128)} %get-tuple-element.189, f32[16,32,2]{2,1,0:T(8,128)} %get-tuple-element.186, ...), kind=kLoop, calls=%fused_computation.375 | loop fusion | flops 1769472 | bytes 2360320 | tf_op jit(solution)/shard_map/add | solution.py:60
  61.7 1.3 collective-permute-start.6
  63.0 3.0 %collective-permute-start.7 = (f32[24,4,128]{2,1,0:T(4,128)S(1)}, f32[24,4,128]{2,1,0:T(4,128)S(1)}, u32[]{:S(2)}, u32[]{:S(2)}) collective-permute-start(f32[24,4,128]{2,1,0:T(4,128)S(1)} %get-tuple-element.171), channel_id=1, source_target_pairs={{0,1},{2,3},{4,5},{6,7},{8,9},{10,11},{12,13},{14,15},{16,17},{18,... | collective-permute-start | bytes 147464 | tf_op jit(solution)/shard_map/ppermute | solution.py:21
  67.2 1.4 collective-permute-start.2
  68.7 3.0 %collective-permute-start.3 = (f32[2,24,4,128]{3,2,1,0:T(4,128)S(1)}, f32[2,24,4,128]{3,2,1,0:T(4,128)S(1)}, u32[]{:S(2)}, u32[]{:S(2)}) collective-permute-start(f32[2,24,4,128]{3,2,1,0:T(4,128)S(1)} %get-tuple-element.77), channel_id=1, source_target_pairs={{0,1},{2,3},{4,5},{6,7},{8,9},{10,11},{12,13},{14,15},{16,17},{18,... | collective-permute-start | bytes 294920 | tf_op jit(solution)/shard_map/ppermute | solution.py:21
  74.2 2.8 %fusion.65 = f32[2,16,32,128]{3,2,1,0:T(8,128)S(1)} fusion(f32[1,16,32,128]{3,2,1,0:T(8,128)S(1)} %get-tuple-element.167, f32[1,16,32,128]{3,2,1,0:T(8,128)S(1)} %get-tuple-element.210, f32[2,16,32,124]{3,2,1,0:T(8,128)S(1)} %copy-done.17, f32[2,16,32,4]{3,2,1,0:T(8,128)S(1)} %copy-done.19, f32[2,16,32,4]{3,2,1,0:T(8,128)S(1)} %copy-done.18, ...), kind=kLoop, calls=%fused_computation.247 | loop fusion | flops 12976128 | bytes 15467520 | tf_op jit(solution)/shard_map/add | solution.py:147
  80.4 15.3 %scatter_fusion = f32[16,32,128]{2,1,0:T(8,128)S(1)} fusion(f32[16,32,128]{2,1,0:T(8,128)S(1)} %get-tuple-element.144, s32[256]{0:T(256)S(1)} %bitcast.108, f32[256]{0:T(256)S(1)} %copy-done.53), kind=kCustom, calls=%fused_computation | custom fusion | flops 256 | bytes 6144 | tf_op jit(solution)/shard_map/scatter-add | solution.py:98
  97.2 4.7 %collective-permute-start.9 = (f32[2,4,32,128]{3,2,1,0:T(8,128)S(1)}, f32[2,4,32,128]{3,2,1,0:T(8,128)S(1)}, u32[]{:S(2)}, u32[]{:S(2)}) collective-permute-start(f32[2,4,32,128]{3,2,1,0:T(8,128)S(1)} %get-tuple-element.126), channel_id=1, source_target_pairs={{0,4},{4,8},{8,12},{1,5},{5,9},{9,13},{2,6},{6,10},{10,14},{3,7},{... | collective-permute-start | bytes 393224 | tf_op jit(solution)/shard_map/ppermute | solution.py:21
  101.9 1.3 collective-permute-start.8
  103.4 0.9 fusion.69
  104.5 4.4 %collective-permute-done.8 = f32[2,4,32,128]{3,2,1,0:T(8,128)S(1)} collective-permute-done((f32[2,4,32,128]{3,2,1,0:T(8,128)S(1)}, f32[2,4,32,128]{3,2,1,0:T(8,128)S(1)}, u32[]{:S(2)}, u32[]{:S(2)}) %collective-permute-start.8) | collective-permute-done | bytes 131104 | tf_op jit(solution)/shard_map/ppermute | solution.py:23
  108.9 1.3 collective-permute-start.10
  110.2 3.0 %collective-permute-start.11 = (f32[2,24,4,128]{3,2,1,0:T(4,128)S(1)}, f32[2,24,4,128]{3,2,1,0:T(4,128)S(1)}, u32[]{:S(2)}, u32[]{:S(2)}) collective-permute-start(f32[2,24,4,128]{3,2,1,0:T(4,128)S(1)} %get-tuple-element.73), channel_id=1, source_target_pairs={{0,1},{2,3},{4,5},{6,7},{8,9},{10,11},{12,13},{14,15},{16,17},{18,... | collective-permute-start | bytes 294920 | tf_op jit(solution)/shard_map/ppermute | solution.py:21
  115.1 2.8 %multiply_add_fusion.2 = f32[2,16,32,128]{3,2,1,0:T(8,128)S(1)} fusion(f32[2,16,32,124]{3,2,1,0:T(8,128)S(1)} %get-tuple-element.141, f32[2,16,32,4]{3,2,1,0:T(8,128)S(1)} %get-tuple-element.143, f32[2,16,32,4]{3,2,1,0:T(8,128)S(1)} %get-tuple-element.142, f32[2,16,32,124]{3,2,1,0:T(8,128)S(1)} %get-tuple-element.140, ...), kind=kLoop, calls=%fused_computation.283 | loop fusion | flops 12976128 | bytes 15467520 | tf_op jit(solution)/shard_map/add | solution.py:147
  121.4 15.3 %scatter_fusion.1 = f32[16,32,128]{2,1,0:T(8,128)S(1)} fusion(f32[16,32,128]{2,1,0:T(8,128)S(1)} %get-tuple-element.122, s32[256]{0:T(256)S(1)} %bitcast.109, f32[256]{0:T(256)S(1)} %copy-done.52), kind=kCustom, calls=%fused_computation.1 | custom fusion | flops 256 | bytes 6144 | tf_op jit(solution)/shard_map/scatter-add | solution.py:98
  138.2 3.7 %collective-permute-start.13 = (f32[2,4,32,128]{3,2,1,0:T(8,128)S(1)}, f32[2,4,32,128]{3,2,1,0:T(8,128)S(1)}, u32[]{:S(2)}, u32[]{:S(2)}) collective-permute-start(f32[2,4,32,128]{3,2,1,0:T(8,128)S(1)} %get-tuple-element.104), channel_id=1, source_target_pairs={{0,4},{4,8},{8,12},{1,5},{5,9},{9,13},{2,6},{6,10},{10,14},{3,7},{... | collective-permute-start | bytes 393224 | tf_op jit(solution)/shard_map/ppermute | solution.py:21
  141.9 1.3 collective-permute-start.12
  143.4 0.9 fusion.68
  144.3 0.9 collective-permute-done.13
  145.2 4.1 %collective-permute-done.12 = f32[2,4,32,128]{3,2,1,0:T(8,128)S(1)} collective-permute-done((f32[2,4,32,128]{3,2,1,0:T(8,128)S(1)}, f32[2,4,32,128]{3,2,1,0:T(8,128)S(1)}, u32[]{:S(2)}, u32[]{:S(2)}) %collective-permute-start.12) | collective-permute-done | bytes 131104 | tf_op jit(solution)/shard_map/ppermute | solution.py:23
  149.3 1.3 collective-permute-start.14
  150.6 3.0 %collective-permute-start.15 = (f32[2,24,4,128]{3,2,1,0:T(4,128)S(1)}, f32[2,24,4,128]{3,2,1,0:T(4,128)S(1)}, u32[]{:S(2)}, u32[]{:S(2)}) collective-permute-start(f32[2,24,4,128]{3,2,1,0:T(4,128)S(1)} %get-tuple-element.69), channel_id=1, source_target_pairs={{0,1},{2,3},{4,5},{6,7},{8,9},{10,11},{12,13},{14,15},{16,17},{18,... | collective-permute-start | bytes 294920 | tf_op jit(solution)/shard_map/ppermute | solution.py:21
  154.8 2.9 %multiply_add_fusion.1 = f32[2,16,32,128]{3,2,1,0:T(8,128)S(1)} fusion(f32[2,16,32,124]{3,2,1,0:T(8,128)S(1)} %get-tuple-element.119, f32[2,16,32,4]{3,2,1,0:T(8,128)S(1)} %get-tuple-element.121, f32[2,16,32,4]{3,2,1,0:T(8,128)S(1)} %get-tuple-element.120, f32[2,16,32,124]{3,2,1,0:T(8,128)S(1)} %get-tuple-element.118, ...), kind=kLoop, calls=%fused_computation.282 | loop fusion | flops 12976128 | bytes 15467520 | tf_op jit(solution)/shard_map/add | solution.py:147
  161.1 15.3 %scatter_fusion.2 = f32[16,32,128]{2,1,0:T(8,128)S(1)} fusion(f32[16,32,128]{2,1,0:T(8,128)S(1)} %get-tuple-element.100, s32[256]{0:T(256)S(1)} %bitcast.110, f32[256]{0:T(256)S(1)} %copy-done.51), kind=kCustom, calls=%fused_computation.2 | custom fusion | flops 256 | bytes 6144 | tf_op jit(solution)/shard_map/scatter-add | solution.py:98
  176.4 1.1 fusion.9
  177.5 1.1 fusion.4
  178.6 1.1 fusion.5
  179.8 1.1 fusion.12
  180.9 1.1 fusion.13
  182.1 1.2 fusion.8
  183.2 1.1 fusion.1
  184.3 2.1 collective-permute-start.17
  186.5 1.3 collective-permute-start.16
  187.8 1.2 fusion
  189.8 4.1 %collective-permute-done.16 = f32[2,4,32,128]{3,2,1,0:T(8,128)S(1)} collective-permute-done((f32[2,4,32,128]{3,2,1,0:T(8,128)S(1)}, f32[2,4,32,128]{3,2,1,0:T(8,128)S(1)}, u32[]{:S(2)}, u32[]{:S(2)}) %collective-permute-start.16) | collective-permute-done | bytes 131104 | tf_op jit(solution)/shard_map/ppermute | solution.py:23
  193.9 1.4 collective-permute-start.18
  195.4 3.0 %collective-permute-start.19 = (f32[2,24,4,128]{3,2,1,0:T(4,128)S(1)}, f32[2,24,4,128]{3,2,1,0:T(4,128)S(1)}, u32[]{:S(2)}, u32[]{:S(2)}) collective-permute-start(f32[2,24,4,128]{3,2,1,0:T(4,128)S(1)} %get-tuple-element.65), channel_id=1, source_target_pairs={{0,1},{2,3},{4,5},{6,7},{8,9},{10,11},{12,13},{14,15},{16,17},{18,... | collective-permute-start | bytes 294920 | tf_op jit(solution)/shard_map/ppermute | solution.py:21
  200.4 1.1 fusion.88
  201.6 1.4 pad_maximum_fusion.8
  203.8 4.6 %multiply_add_fusion = f32[2,16,32,128]{3,2,1,0:T(8,128)S(1)} fusion(f32[2,16,32,124]{3,2,1,0:T(8,128)} %get-tuple-element.97, f32[2,16,32,4]{3,2,1,0:T(8,128)} %get-tuple-element.99, f32[2,16,32,4]{3,2,1,0:T(8,128)} %get-tuple-element.98, f32[2,16,32,124]{3,2,1,0:T(8,128)} %get-tuple-element.96, f32[2,16,32,125]{3,2,1,0:T(8,128)} %get-tuple-element.93, ...), kind=kLoop, calls=%fused_computation.281 | loop fusion | flops 12976128 | bytes 15467520 | tf_op jit(solution)/shard_map/add | solution.py:147
  211.8 15.3 %scatter_fusion.3 = f32[16,32,128]{2,1,0:T(8,128)S(1)} fusion(f32[16,32,128]{2,1,0:T(8,128)S(1)} %get-tuple-element.78, s32[256]{0:T(256)S(1)} %bitcast.111, f32[256]{0:T(256)S(1)} %copy-done.50), kind=kCustom, calls=%fused_computation.3 | custom fusion | flops 256 | bytes 6144 | tf_op jit(solution)/shard_map/scatter-add | solution.py:98
  229.1 1.6 multiply_subtract_fusion
  (200 shorter events, 32.9 us)
Async XLA Ops:
  7.2 40.3 %copy-start = (f32[4,4]{1,0:T(4,128)S(1)}, f32[4,4]{1,0:T(4,128)}, u32[]{:S(2)}) copy-start(f32[4,4]{1,0:T(4,128)} %param.25) | copy-start | bytes 196
  7.2 221.6 %reduce-scatter.2.cloned.1.call-start = ((), (), s32[]{:S(2)}) async-start(), calls=%async_computation.1 | async-start | bytes 393216 | tf_op jit(solution)/shard_map/reduce_scatter | solution.py:165
  8.8 52.0 %collective-permute-start.4 = (f32[4,32,128]{2,1,0:T(8,128)}, f32[4,32,128]{2,1,0:T(8,128)}, u32[]{:S(2)}, u32[]{:S(2)}) collective-permute-start(f32[4,32,128]{2,1,0:T(8,128)} %get-tuple-element.175), channel_id=1, source_target_pairs={{4,0},{8,4},{12,8},{5,1},{9,5},{13,9},{6,2},{10,6},{14,10},{7,3},{... | collective-permute-start | bytes 196616 | tf_op jit(solution)/shard_map/ppermute | solution.py:23
  10.0 49.8 %collective-permute-start.5 = (f32[4,32,128]{2,1,0:T(8,128)}, f32[4,32,128]{2,1,0:T(8,128)}, u32[]{:S(2)}, u32[]{:S(2)}) collective-permute-start(f32[4,32,128]{2,1,0:T(8,128)} %get-tuple-element.176), channel_id=1, source_target_pairs={{0,4},{4,8},{8,12},{1,5},{5,9},{9,13},{2,6},{6,10},{10,14},{3,7},{... | collective-permute-start | bytes 196616 | tf_op jit(solution)/shard_map/ppermute | solution.py:21
  17.5 14.6 %copy-start.2 = (f32[16,32,128]{2,1,0:T(8,128)S(1)}, f32[16,32,128]{2,1,0:T(8,128)}, u32[]{:S(2)}) copy-start(f32[16,32,128]{2,1,0:T(8,128)} %param.20) | copy-start | bytes 786436
  18.2 48.9 %collective-permute-start.1 = (f32[2,4,32,128]{3,2,1,0:T(8,128)}, f32[2,4,32,128]{3,2,1,0:T(8,128)S(1)}, u32[]{:S(2)}, u32[]{:S(2)}) collective-permute-start(f32[2,4,32,128]{3,2,1,0:T(8,128)} %get-tuple-element.148), channel_id=1, source_target_pairs={{0,4},{4,8},{8,12},{1,5},{5,9},{9,13},{2,6},{6,10},{10,14},{3,7},{... | collective-permute-start | bytes 393224 | tf_op jit(solution)/shard_map/ppermute | solution.py:21
  21.5 45.7 %collective-permute-start = (f32[2,4,32,128]{3,2,1,0:T(8,128)S(1)}, f32[2,4,32,128]{3,2,1,0:T(8,128)S(1)}, u32[]{:S(2)}, u32[]{:S(2)}) collective-permute-start(f32[2,4,32,128]{3,2,1,0:T(8,128)S(1)} %get-tuple-element.149), channel_id=1, source_target_pairs={{4,0},{8,4},{12,8},{5,1},{9,5},{13,9},{6,2},{10,6},{14,10},{7,3},{... | collective-permute-start | bytes 393224 | tf_op jit(solution)/shard_map/ppermute | solution.py:23
  46.4 4.2 %copy-start.6 = (bf16[1,6,16,32,128]{4,3,2,1,0:T(8,128)(2,1)S(1)}, bf16[1,6,16,32,128]{4,3,2,1,0:T(8,128)(2,1)}, u32[]{:S(2)}) copy-start(bf16[1,6,16,32,128]{4,3,2,1,0:T(8,128)(2,1)} %param.23) | copy-start | bytes 2359300
  56.4 2.7 %copy-start.55 = (s32[3]{0:T(128)S(1)}, s32[3]{0:T(128)}, u32[]{:S(2)}) copy-start(s32[3]{0:T(128)} %constant.323.clone.1) | copy-start | bytes 40
  61.7 4.5 %collective-permute-start.6 = (f32[24,4,128]{2,1,0:T(4,128)S(1)}, f32[24,4,128]{2,1,0:T(4,128)S(1)}, u32[]{:S(2)}, u32[]{:S(2)}) collective-permute-start(f32[24,4,128]{2,1,0:T(4,128)S(1)} %get-tuple-element.170), channel_id=1, source_target_pairs={{1,0},{3,2},{5,4},{7,6},{9,8},{11,10},{13,12},{15,14},{17,16},{19,... | collective-permute-start | bytes 147464 | tf_op jit(solution)/shard_map/ppermute | solution.py:23
  63.0 3.9 %collective-permute-start.7 = (f32[24,4,128]{2,1,0:T(4,128)S(1)}, f32[24,4,128]{2,1,0:T(4,128)S(1)}, u32[]{:S(2)}, u32[]{:S(2)}) collective-permute-start(f32[24,4,128]{2,1,0:T(4,128)S(1)} %get-tuple-element.171), channel_id=1, source_target_pairs={{0,1},{2,3},{4,5},{6,7},{8,9},{10,11},{12,13},{14,15},{16,17},{18,... | collective-permute-start | bytes 147464 | tf_op jit(solution)/shard_map/ppermute | solution.py:21
  66.0 6.8 %copy-start.23 = (f32[2,16,32,1]{3,2,1,0:T(8,128)S(1)}, f32[2,16,32,1]{3,2,1,0:T(8,128)}, u32[]{:S(2)}) copy-start(f32[2,16,32,1]{3,2,1,0:T(8,128)} %get-tuple-element.153) | copy-start | bytes 12292
  66.0 6.8 %copy-start.24 = (f32[2,16,32,127]{3,2,1,0:T(8,128)S(1)}, f32[2,16,32,127]{3,2,1,0:T(8,128)}, u32[]{:S(2)}) copy-start(f32[2,16,32,127]{3,2,1,0:T(8,128)} %get-tuple-element.150) | copy-start | bytes 1560580
  66.0 6.8 %copy-start.25 = (f32[2,16,32,127]{3,2,1,0:T(8,128)S(1)}, f32[2,16,32,127]{3,2,1,0:T(8,128)}, u32[]{:S(2)}) copy-start(f32[2,16,32,127]{3,2,1,0:T(8,128)} %get-tuple-element.151) | copy-start | bytes 1560580
  66.9 6.0 %copy-start.22 = (f32[2,16,32,1]{3,2,1,0:T(8,128)S(1)}, f32[2,16,32,1]{3,2,1,0:T(8,128)}, u32[]{:S(2)}) copy-start(f32[2,16,32,1]{3,2,1,0:T(8,128)} %get-tuple-element.152) | copy-start | bytes 12292
  67.2 5.7 %copy-start.20 = (f32[2,16,32,125]{3,2,1,0:T(8,128)S(1)}, f32[2,16,32,125]{3,2,1,0:T(8,128)}, u32[]{:S(2)}) copy-start(f32[2,16,32,125]{3,2,1,0:T(8,128)} %get-tuple-element.158) | copy-start | bytes 1536004
  67.2 5.7 %copy-start.21 = (f32[2,16,32,125]{3,2,1,0:T(8,128)S(1)}, f32[2,16,32,125]{3,2,1,0:T(8,128)}, u32[]{:S(2)}) copy-start(f32[2,16,32,125]{3,2,1,0:T(8,128)} %get-tuple-element.159) | copy-start | bytes 1536004
  67.2 4.7 %collective-permute-start.2 = (f32[2,24,4,128]{3,2,1,0:T(4,128)S(1)}, f32[2,24,4,128]{3,2,1,0:T(4,128)S(1)}, u32[]{:S(2)}, u32[]{:S(2)}) collective-permute-start(f32[2,24,4,128]{3,2,1,0:T(4,128)S(1)} %get-tuple-element.76), channel_id=1, source_target_pairs={{1,0},{3,2},{5,4},{7,6},{9,8},{11,10},{13,12},{15,14},{17,16},{19,... | collective-permute-start | bytes 294920 | tf_op jit(solution)/shard_map/ppermute | solution.py:23
  68.7 4.0 %collective-permute-start.3 = (f32[2,24,4,128]{3,2,1,0:T(4,128)S(1)}, f32[2,24,4,128]{3,2,1,0:T(4,128)S(1)}, u32[]{:S(2)}, u32[]{:S(2)}) collective-permute-start(f32[2,24,4,128]{3,2,1,0:T(4,128)S(1)} %get-tuple-element.77), channel_id=1, source_target_pairs={{0,1},{2,3},{4,5},{6,7},{8,9},{10,11},{12,13},{14,15},{16,17},{18,... | collective-permute-start | bytes 294920 | tf_op jit(solution)/shard_map/ppermute | solution.py:21
  71.7 1.2 copy-start.16
  71.7 1.2 copy-start.17
  71.8 1.3 copy-start.18
  71.8 1.5 copy-start.19
  71.9 1.4 copy-start.3
  71.9 1.6 copy-start.11
  71.9 1.7 copy-start.12
  72.0 1.9 copy-start.13
  72.0 2.0 copy-start.14
  72.0 2.2 copy-start.15
  72.8 1.4 copy-start.46
  72.8 1.4 copy-start.48
  97.2 7.3 %collective-permute-start.9 = (f32[2,4,32,128]{3,2,1,0:T(8,128)S(1)}, f32[2,4,32,128]{3,2,1,0:T(8,128)S(1)}, u32[]{:S(2)}, u32[]{:S(2)}) collective-permute-start(f32[2,4,32,128]{3,2,1,0:T(8,128)S(1)} %get-tuple-element.126), channel_id=1, source_target_pairs={{0,4},{4,8},{8,12},{1,5},{5,9},{9,13},{2,6},{6,10},{10,14},{3,7},{... | collective-permute-start | bytes 393224 | tf_op jit(solution)/shard_map/ppermute | solution.py:21
  101.9 7.0 %collective-permute-start.8 = (f32[2,4,32,128]{3,2,1,0:T(8,128)S(1)}, f32[2,4,32,128]{3,2,1,0:T(8,128)S(1)}, u32[]{:S(2)}, u32[]{:S(2)}) collective-permute-start(f32[2,4,32,128]{3,2,1,0:T(8,128)S(1)} %get-tuple-element.127), channel_id=1, source_target_pairs={{4,0},{8,4},{12,8},{5,1},{9,5},{13,9},{6,2},{10,6},{14,10},{7,3},{... | collective-permute-start | bytes 393224 | tf_op jit(solution)/shard_map/ppermute | solution.py:23
  108.9 4.5 %collective-permute-start.10 = (f32[2,24,4,128]{3,2,1,0:T(4,128)S(1)}, f32[2,24,4,128]{3,2,1,0:T(4,128)S(1)}, u32[]{:S(2)}, u32[]{:S(2)}) collective-permute-start(f32[2,24,4,128]{3,2,1,0:T(4,128)S(1)} %get-tuple-element.72), channel_id=1, source_target_pairs={{1,0},{3,2},{5,4},{7,6},{9,8},{11,10},{13,12},{15,14},{17,16},{19,... | collective-permute-start | bytes 294920 | tf_op jit(solution)/shard_map/ppermute | solution.py:23
  110.2 4.0 %collective-permute-start.11 = (f32[2,24,4,128]{3,2,1,0:T(4,128)S(1)}, f32[2,24,4,128]{3,2,1,0:T(4,128)S(1)}, u32[]{:S(2)}, u32[]{:S(2)}) collective-permute-start(f32[2,24,4,128]{3,2,1,0:T(4,128)S(1)} %get-tuple-element.73), channel_id=1, source_target_pairs={{0,1},{2,3},{4,5},{6,7},{8,9},{10,11},{12,13},{14,15},{16,17},{18,... | collective-permute-start | bytes 294920 | tf_op jit(solution)/shard_map/ppermute | solution.py:21
  138.2 7.0 %collective-permute-start.13 = (f32[2,4,32,128]{3,2,1,0:T(8,128)S(1)}, f32[2,4,32,128]{3,2,1,0:T(8,128)S(1)}, u32[]{:S(2)}, u32[]{:S(2)}) collective-permute-start(f32[2,4,32,128]{3,2,1,0:T(8,128)S(1)} %get-tuple-element.104), channel_id=1, source_target_pairs={{0,4},{4,8},{8,12},{1,5},{5,9},{9,13},{2,6},{6,10},{10,14},{3,7},{... | collective-permute-start | bytes 393224 | tf_op jit(solution)/shard_map/ppermute | solution.py:21
  141.9 7.4 %collective-permute-start.12 = (f32[2,4,32,128]{3,2,1,0:T(8,128)S(1)}, f32[2,4,32,128]{3,2,1,0:T(8,128)S(1)}, u32[]{:S(2)}, u32[]{:S(2)}) collective-permute-start(f32[2,4,32,128]{3,2,1,0:T(8,128)S(1)} %get-tuple-element.105), channel_id=1, source_target_pairs={{4,0},{8,4},{12,8},{5,1},{9,5},{13,9},{6,2},{10,6},{14,10},{7,3},{... | collective-permute-start | bytes 393224 | tf_op jit(solution)/shard_map/ppermute | solution.py:23
  149.3 4.5 %collective-permute-start.14 = (f32[2,24,4,128]{3,2,1,0:T(4,128)S(1)}, f32[2,24,4,128]{3,2,1,0:T(4,128)S(1)}, u32[]{:S(2)}, u32[]{:S(2)}) collective-permute-start(f32[2,24,4,128]{3,2,1,0:T(4,128)S(1)} %get-tuple-element.68), channel_id=1, source_target_pairs={{1,0},{3,2},{5,4},{7,6},{9,8},{11,10},{13,12},{15,14},{17,16},{19,... | collective-permute-start | bytes 294920 | tf_op jit(solution)/shard_map/ppermute | solution.py:23
  150.6 4.0 %collective-permute-start.15 = (f32[2,24,4,128]{3,2,1,0:T(4,128)S(1)}, f32[2,24,4,128]{3,2,1,0:T(4,128)S(1)}, u32[]{:S(2)}, u32[]{:S(2)}) collective-permute-start(f32[2,24,4,128]{3,2,1,0:T(4,128)S(1)} %get-tuple-element.69), channel_id=1, source_target_pairs={{0,1},{2,3},{4,5},{6,7},{8,9},{10,11},{12,13},{14,15},{16,17},{18,... | collective-permute-start | bytes 294920 | tf_op jit(solution)/shard_map/ppermute | solution.py:21
  184.3 5.4 %collective-permute-start.17 = (f32[2,4,32,128]{3,2,1,0:T(8,128)S(1)}, f32[2,4,32,128]{3,2,1,0:T(8,128)S(1)}, u32[]{:S(2)}, u32[]{:S(2)}) collective-permute-start(f32[2,4,32,128]{3,2,1,0:T(8,128)S(1)} %get-tuple-element.82), channel_id=1, source_target_pairs={{0,4},{4,8},{8,12},{1,5},{5,9},{9,13},{2,6},{6,10},{10,14},{3,7},{... | collective-permute-start | bytes 393224 | tf_op jit(solution)/shard_map/ppermute | solution.py:21
  186.5 7.4 %collective-permute-start.16 = (f32[2,4,32,128]{3,2,1,0:T(8,128)S(1)}, f32[2,4,32,128]{3,2,1,0:T(8,128)S(1)}, u32[]{:S(2)}, u32[]{:S(2)}) collective-permute-start(f32[2,4,32,128]{3,2,1,0:T(8,128)S(1)} %get-tuple-element.83), channel_id=1, source_target_pairs={{4,0},{8,4},{12,8},{5,1},{9,5},{13,9},{6,2},{10,6},{14,10},{7,3},{... | collective-permute-start | bytes 393224 | tf_op jit(solution)/shard_map/ppermute | solution.py:23
  193.9 5.4 %copy-start.31 = (f32[2,4,32,128]{3,2,1,0:T(8,128)}, f32[2,4,32,128]{3,2,1,0:T(8,128)S(1)}, u32[]{:S(2)}) copy-start(f32[2,4,32,128]{3,2,1,0:T(8,128)S(1)} %collective-permute-done.16) | copy-start | bytes 393220
  193.9 6.1 %copy-start.32 = (f32[24,40,128]{2,1,0:T(8,128)S(1)}, f32[24,40,128]{2,1,0:T(8,128)}, u32[]{:S(2)}) copy-start(f32[24,40,128]{2,1,0:T(8,128)} %fusion.69) | copy-start | bytes 1474564
  193.9 6.1 %copy-start.33 = (f32[24,40,128]{2,1,0:T(8,128)S(1)}, f32[24,40,128]{2,1,0:T(8,128)}, u32[]{:S(2)}) copy-start(f32[24,40,128]{2,1,0:T(8,128)} %fusion.68) | copy-start | bytes 1474564
  193.9 4.7 %collective-permute-start.18 = (f32[2,24,4,128]{3,2,1,0:T(4,128)S(1)}, f32[2,24,4,128]{3,2,1,0:T(4,128)S(1)}, u32[]{:S(2)}, u32[]{:S(2)}) collective-permute-start(f32[2,24,4,128]{3,2,1,0:T(4,128)S(1)} %get-tuple-element.64), channel_id=1, source_target_pairs={{1,0},{3,2},{5,4},{7,6},{9,8},{11,10},{13,12},{15,14},{17,16},{19,... | collective-permute-start | bytes 294920 | tf_op jit(solution)/shard_map/ppermute | solution.py:23
  195.4 4.0 %collective-permute-start.19 = (f32[2,24,4,128]{3,2,1,0:T(4,128)S(1)}, f32[2,24,4,128]{3,2,1,0:T(4,128)S(1)}, u32[]{:S(2)}, u32[]{:S(2)}) collective-permute-start(f32[2,24,4,128]{3,2,1,0:T(4,128)S(1)} %get-tuple-element.65), channel_id=1, source_target_pairs={{0,1},{2,3},{4,5},{6,7},{8,9},{10,11},{12,13},{14,15},{16,17},{18,... | collective-permute-start | bytes 294920 | tf_op jit(solution)/shard_map/ppermute | solution.py:21
  198.4 1.6 copy-start.8
  198.4 1.6 copy-start.9
  198.4 1.6 copy-start.10
  198.6 1.8 copy-start.7
  198.6 0.8 copy-start.34
  201.5 1.5 copy-start.4
  201.5 1.5 copy-start.26
  201.6 1.5 copy-start.27
  201.6 1.6 copy-start.28
  201.6 1.8 copy-start.29
  201.6 1.9 copy-start.30
  201.6 1.9 copy-start.47
  201.6 1.9 copy-start.49
  203.0 0.7 copy-start.39
  203.0 0.8 copy-start.42
  203.0 0.8 copy-start.45
  227.9 1.0 copy-start.5
  227.9 1.2 copy-start.36
  (14 other events, 9.1 us)
Sparse Core Ops, SparseCore 0:
  201.6 9.9 reduce-scatter.1
where the time goes:
time: 239 us; the launch traced here: 238 us
  other arithmetic  114 us (48%)
  starting transfers between devices  48.5 us (20%)
  between operations  31.8 us (13%)
  local copies, waits for them, and re-layouts  25.5 us (11%)
  waiting for transfers between devices  18.1 us (8%)
    scatter-add x4, other arithmetic, place_values(): field.at[depth_safe, row_safe, column_index]  61 us
    ppermute x10, starting transfers between devices, extended(): lax.ppermute(tail, axis, [(i, (i + 1) % count) for i in range(ends)])  35.2 us
    ppermute x10, starting transfers between devices, extended(): lax.ppermute(head, axis, [((i + 1) % count, i) for i in range(ends)])  13.2 us
    add x4, other arithmetic, local(): 2.0 * trim(current_ext, 4) - prev_core  13 us
    ppermute x10, waiting for transfers between devices, extended(): lax.ppermute(head, axis, [((i + 1) % count, i) for i in range(ends)])  12.7 us
    another operation x27, other arithmetic, local(): current = jnp.stack([fwd_next, adj_next])  12.6 us
    another operation x9, other arithmetic, local(): current = jnp.stack([forward_pair[0, 1], adjoint_pair[0, 1]])  9.73 us
    unnamed x116, local copies, waits for them, and re-layouts  9.6 us
  transfers between devices with their start and end apart: 21, of which 11 were waited for; matrix products, arithmetic and copies ran while one was open for 25% of the time, Pallas kernels for 0%

commit v1 on v0

v1 whole, which is shorter than its diff:
```python
import functools
import jax
import jax.numpy as jnp
from jax import lax
from jax.experimental import pallas as pl
from jax.experimental.pallas import tpu as pltpu
from jax.sharding import PartitionSpec as P

SECOND_TAPS = (8.0 / 5.0, -1.0 / 5.0, 8.0 / 315.0, -1.0 / 560.0)
CENTER_TAP = -205.0 / 72.0
FIRST_TAPS = (4.0 / 5.0, -1.0 / 5.0, 4.0 / 105.0, -1.0 / 280.0)
MOMENT_KEEP = 0.9
STEP_RATE = 0.02
MESH = pl.DeviceIdType.MESH
BF = jnp.bfloat16
F32 = jnp.float32
FWD, ADJ = 0, 1


def split_div(value, size):
    if size & (size - 1) == 0:
        bits = size.bit_length() - 1
        return lax.shift_right_logical(value, bits), value & (size - 1)
    whole = lax.div(value, size)
    return whole, value - whole * size


def kernel(
    dims,
    assign_ref, source_ref, wave_ref, recv_ref, resid_ref,
    model_ref, buoy_ref, fpair_ref, apair_ref, states_ref, mom_ref,
    fout_ref, aout_ref, momout_ref, modout_ref,
    ext, bext, model_v, states_v, mom_v, coef, inj, xder, img, share, momnew, modnew, wmat,
    zsend, zrecv, ysend, yrecv, bsend, brecv, ssend, srecv, load, store,
):
    groups, n_depth, n_lat, planes, rows, cols, steps, n_rec = dims
    rows_all = rows * n_lat
    q = planes // groups
    d = lax.axis_index("depth")
    l = lax.axis_index("lat")
    s = lax.axis_index("shot")
    pairs = (fpair_ref, apair_ref)
    core_p = pl.ds(4, planes)
    core_r = pl.ds(8, rows)
    has = {
        ("depth", 0): d > 0,
        ("depth", 1): d < n_depth - 1,
        ("lat", 0): l > 0,
        ("lat", 1): l < n_lat - 1,
    }
    rank = {"depth": d, "lat": l}

    loads = {}

    def begin(name, src, dst):
        loads[name] = pltpu.make_async_copy(src, dst, load.at[len(loads)])
        loads[name].start()

    begin("buoy", buoy_ref, bext.at[core_p, core_r])
    begin("model", model_ref, model_v)
    for f in (ADJ, FWD):
        begin(("cur", f), pairs[f].at[0, 1], ext.at[0, f, core_p, core_r])
        begin(("prev", f), pairs[f].at[0, 0], ext.at[1, f, core_p, core_r])
    begin("states", states_ref.at[0], states_v)
    begin("mom", mom_ref, mom_v)

    for lo in (0, planes + 4):
        for slot in range(2):
            for f in range(2):
                ext[slot, f, pl.ds(lo, 4), core_r] = jnp.zeros((4, rows, cols), F32)
        bext[pl.ds(lo, 4), core_r] = jnp.zeros((4, rows, cols), F32)
    for lo in (0, rows + 8):
        for slot in range(2):
            for f in range(2):
                ext[slot, f, core_p, pl.ds(lo, 8)] = jnp.zeros((planes, 8, cols), F32)
        bext[core_p, pl.ds(lo, 8)] = jnp.zeros((planes, 8, cols), F32)

    barrier = pltpu.get_barrier_semaphore()
    total = groups - 1
    for (axis, way), there in has.items():
        total = total + there.astype(jnp.int32)

        @pl.when(there)
        def _(axis=axis, way=way):
            pl.semaphore_signal(
                barrier, inc=1, device_id={axis: rank[axis] + 2 * way - 1}, device_id_type=MESH
            )

    for o in range(1, groups):
        pl.semaphore_signal(
            barrier, inc=1, device_id={"shot": lax.rem(s + o, groups)}, device_id_type=MESH
        )
    pl.semaphore_wait(barrier, total)

    def remote(src, dst, send, recv, axis, way):
        return pltpu.make_async_remote_copy(
            src_ref=src, dst_ref=dst, send_sem=send, recv_sem=recv,
            device_id={axis: rank[axis] + 2 * way - 1}, device_id_type=MESH,
        )

    chunks = ((0, 4), (planes - 4, 4)) + (((4, planes - 8),) if planes > 8 else ())

    def zcopy(e, f, way):
        slot = e % 2
        first = planes - 4 if way else 0
        if e == 0:
            src = pairs[f].at[0, 1, pl.ds(first, 4)]
        else:
            src = ext.at[slot, f, pl.ds(4 + first, 4), core_r]
        dst = ext.at[slot, f, pl.ds(0 if way else planes + 4, 4), core_r]
        return remote(src, dst, zsend.at[e, f, way], zrecv.at[e, f, way], "depth", way)

    def ycopy(e, f, c, way):
        slot = e % 2
        first, count = chunks[c]
        row = rows - 8 if way else 0
        if e == 0:
            src = pairs[f].at[0, 1, pl.ds(first, count), pl.ds(row, 8)]
        else:
            src = ext.at[slot, f, pl.ds(4 + first, count), pl.ds(8 + row, 8)]
        dst = ext.at[slot, f, pl.ds(4 + first, count), pl.ds(0 if way else rows + 8, 8)]
        return remote(src, dst, ysend.at[e, f, c, way], yrecv.at[e, f, c, way], "lat", way)

    def bcopy(axis, way):
        a = 0 if axis == "depth" else 1
        if a == 0:
            src = buoy_ref.at[pl.ds(planes - 4 if way else 0, 4)]
            dst = bext.at[pl.ds(0 if way else planes + 4, 4), core_r]
        else:
            src = buoy_ref.at[:, pl.ds(rows - 8 if way else 0, 8)]
            dst = bext.at[core_p, pl.ds(0 if way else rows + 8, 8)]
        return remote(src, dst, bsend.at[a, way], brecv.at[a, way], axis, way)

    def start(copy, axis, way):
        @pl.when(has[(axis, way)])
        def _():
            copy.start()

    def wait_send(copy, axis, way):
        @pl.when(has[(axis, way)])
        def _():
            copy.wait_send()

    def wait_recv(copy, axis, way):
        @pl.when(has[(axis, 1 - way)])
        def _():
            copy.wait_recv()

    for way in (0, 1):
        start(bcopy("depth", way), "depth", way)
        start(bcopy("lat", way), "lat", way)
    for f in (ADJ, FWD):
        for way in (0, 1):
            start(zcopy(0, f, way), "depth", way)
            for c in range(len(chunks)):
                start(ycopy(0, f, c, way), "lat", way)

    delta = lax.broadcasted_iota(jnp.int32, (cols, cols), 0) - lax.broadcasted_iota(
        jnp.int32, (cols, cols), 1
    )
    second = jnp.where(delta == 0, 3.0 * CENTER_TAP, 0.0).astype(F32)
    first = jnp.zeros((cols, cols), F32)
    for reach in range(1, 5):
        second = jnp.where(jnp.abs(delta) == reach, SECOND_TAPS[reach - 1], second)
        first = jnp.where(delta == reach, FIRST_TAPS[reach - 1], first)
        first = jnp.where(delta == -reach, -FIRST_TAPS[reach - 1], first)
    for a, mat in ((0, second), (1, first)):
        high = mat.astype(BF)
        low = (mat - high.astype(F32)).astype(BF)
        wmat[pl.ds(0, cols), pl.ds(a * cols, cols)] = high
        wmat[pl.ds(cols, cols), pl.ds(a * cols, cols)] = high
        wmat[pl.ds(2 * cols, cols), pl.ds(a * cols, cols)] = low

    fshot = assign_ref[s]
    ashot = assign_ref[groups + s]
    cells = recv_ref[pl.ds(ashot, 1), :]
    line, column = split_div(cells, cols)
    depth_id, row_id = split_div(line, rows_all)
    depth_id = depth_id - d * planes
    row_id = row_id - l * rows
    inside = (depth_id >= 0) & (depth_id < planes) & (row_id >= 0) & (row_id < rows)
    where_row = jnp.where(inside, depth_id * rows + row_id, -1)
    row_hot = jnp.where(
        lax.broadcasted_iota(jnp.int32, (planes * rows, n_rec), 0) == where_row, 1.0, 0.0
    ).astype(BF)
    col_hit = lax.broadcasted_iota(jnp.int32, (cols, n_rec), 0) == column
    traces = resid_ref[ashot]
    contract = (((1,), (1,)), ((), ()))
    for k in range(steps):
        part = jnp.where(col_hit, traces[k : k + 1, :], 0.0)
        amount = None
        for _ in range(3):
            piece = part.astype(BF)
            part = part - piece.astype(F32)
            term = lax.dot_general(row_hot, piece, contract, preferred_element_type=F32)
            amount = term if amount is None else amount + term
        inj[k] = amount.reshape(planes, rows, cols)

    sline, scol = split_div(source_ref[fshot], cols)
    sdepth, srow = split_div(sline, rows_all)
    sdepth = sdepth - d * planes
    srow = srow - l * rows
    sinside = (srow >= 0) & (srow < rows)
    sdepth = jnp.where(sinside, sdepth, -1)
    cell_ids = lax.broadcasted_iota(jnp.int32, (rows, cols), 0) * cols + lax.broadcasted_iota(
        jnp.int32, (rows, cols), 1
    )
    scell = srow * cols + scol

    def x_part(block):
        count = block.shape[0]
        block = block.reshape(count * rows, cols)
        high = block.astype(BF)
        low = (block - high.astype(F32)).astype(BF)
        lhs = jnp.concatenate([high, low, high], axis=1)
        return jnp.dot(lhs, wmat[...], preferred_element_type=F32)

    def imaging(k):
        def body(p, carry):
            older = states_v[k, p].astype(F32)
            mid = states_v[k + 1, p].astype(F32)
            newer = states_v[k + 2, p].astype(F32)
            term = ext[k % 2, ADJ, p + 4, core_r] * (newer - 2.0 * mid + older)
            img[p] = term if k == 0 else img[p] + term
            return carry

        lax.fori_loop(0, planes, body, 0)

    def diffs(pick, want_second):
        first = None
        second = None
        for reach in range(1, 5):
            ahead, behind = pick(reach), pick(-reach)
            term = FIRST_TAPS[reach - 1] * (ahead - behind)
            first = term if first is None else first + term
            if want_second:
                term = SECOND_TAPS[reach - 1] * (ahead + behind)
                second = term if second is None else second + term
        return first, second

    def coefficients(p0):
        xs = x_part(bext[pl.ds(p0 + 4, 4), core_r])
        for i in range(4):
            p = p0 + i
            m = model_v[p]
            sz, _ = diffs(lambda o: bext[p + 4 + o, core_r], False)
            sy, _ = diffs(lambda o: bext[p + 4, pl.ds(8 + o, rows)], False)
            coef[0, p] = m * bext[p + 4, core_r]
            coef[1, p] = m * sz
            coef[2, p] = m * sy
            coef[3, p] = m * xs[i * rows : (i + 1) * rows, cols:]

    def advance(k, f, p0):
        now, then = k % 2, (k + 1) % 2
        xder[...] = x_part(ext[now, f, pl.ds(p0 + 4, 4), core_r])
        for i in range(4):
            p = p0 + i
            fz, gz = diffs(lambda o: ext[now, f, p + 4 + o, core_r], True)
            fy, gy = diffs(lambda o: ext[now, f, p + 4, pl.ds(8 + o, rows)], True)
            xrow = pl.ds(i * rows, rows)
            second = gz + gy + xder[xrow, pl.ds(0, cols)]
            value = (
                2.0 * ext[now, f, p + 4, core_r]
                - ext[then, f, p + 4, core_r]
                + coef[0, p] * second
                + coef[1, p] * fz
                + coef[2, p] * fy
                + coef[3, p] * xder[xrow, pl.ds(cols, cols)]
            )
            if f == ADJ:
                value = value + inj[k, p]
            else:
                here = jnp.where(sdepth == p, scell, -1)
                value = value + jnp.where(cell_ids == here, wave_ref[fshot, k], 0.0)
            ext[then, f, p + 4, core_r] = value

    loads["states"].wait()
    loads[("cur", ADJ)].wait()
    imaging(0)
    loads["model"].wait()
    loads["buoy"].wait()
    for way in (0, 1):
        wait_recv(bcopy("lat", way), "lat", way)
        wait_recv(bcopy("depth", way), "depth", way)

    def coef_body(c, carry):
        coefficients(c * 4)
        return carry

    lax.fori_loop(0, planes // 4, coef_body, 0)
    loads[("prev", ADJ)].wait()
    loads[("cur", FWD)].wait()
    loads[("prev", FWD)].wait()

    outs = (fout_ref, aout_ref)
    finals = []

    def share_copy(o):
        dest = lax.rem(s + o, groups)
        return pltpu.make_async_remote_copy(
            src_ref=img.at[pl.ds(dest * q, q)], dst_ref=share.at[o - 1],
            send_sem=ssend.at[o - 1], recv_sem=srecv.at[o - 1],
            device_id={"shot": dest}, device_id_type=MESH,
        )

    def finish(src, dst):
        copy = pltpu.make_async_copy(src, dst, store.at[len(finals)])
        copy.start()
        finals.append(copy)

    for k in range(steps):
        last = k == steps - 1
        if k > 0:
            imaging(k)
        if last:
            for o in range(1, groups):
                share_copy(o).start()
            for f in (ADJ, FWD):
                finish(ext.at[k % 2, f, core_p, core_r], outs[f].at[0, 0])
        for f in (ADJ, FWD):
            if k >= 2:
                for way in (0, 1):
                    wait_send(zcopy(k - 1, f, way), "depth", way)
                    for c in range(len(chunks)):
                        wait_send(ycopy(k - 1, f, c, way), "lat", way)
            for c in (0, 1):
                for way in (0, 1):
                    wait_recv(ycopy(k, f, c, way), "lat", way)
                wait_recv(zcopy(k, f, 1 - c), "depth", 1 - c)
                advance(k, f, chunks[c][0])
                if not last:
                    start(zcopy(k + 1, f, c), "depth", c)
                    for way in (0, 1):
                        start(ycopy(k + 1, f, c, way), "lat", way)
        for f in (ADJ, FWD):
            if len(chunks) > 2:
                for way in (0, 1):
                    wait_recv(ycopy(k, f, 2, way), "lat", way)

                def inner(c, carry):
                    advance(k, f, 4 + c * 4)
                    return carry

                lax.fori_loop(0, (planes - 8) // 4, inner, 0)
                if not last:
                    for way in (0, 1):
                        start(ycopy(k + 1, f, 2, way), "lat", way)
            if last:
                finish(ext.at[(k + 1) % 2, f, core_p, core_r], outs[f].at[0, 1])

    loads["mom"].wait()
    for o in range(1, groups):
        share_copy(o).wait_recv()
    factor = 1.0 / (groups * steps)
    for p in range(q):
        gradient = img[s * q + p]
        for o in range(1, groups):
            gradient = gradient + share[o - 1, p]
        moment = MOMENT_KEEP * mom_v[p] + factor * gradient
        momnew[p] = moment
        modnew[p] = model_v[s * q + p] - STEP_RATE * moment
    finish(momnew, momout_ref)
    finish(modnew, modout_ref)
    for o in range(1, groups):
        share_copy(o).wait_send()
    for way in (0, 1):
        wait_send(bcopy("depth", way), "depth", way)
        wait_send(bcopy("lat", way), "lat", way)
    for e in sorted({0, steps - 1}):
        for f in (ADJ, FWD):
            for way in (0, 1):
                wait_send(zcopy(e, f, way), "depth", way)
                for c in range(len(chunks)):
                    wait_send(ycopy(e, f, c, way), "lat", way)
    for copy in finals:
        copy.wait()


def local(
    model_field, buoyancy, forward_pair, adjoint_pair, stored_states, momentum,
    wavelet, residuals, source_cells, receiver_cells, assignment,
):
    groups = lax.axis_size("shot")
    n_depth = lax.axis_size("depth")
    n_lat = lax.axis_size("lat")
    planes, rows, cols = model_field.shape
    steps = stored_states.shape[1] - 2
    n_rec = receiver_cells.shape[1]
    q = planes // groups
    dims = (groups, n_depth, n_lat, planes, rows, cols, steps, n_rec)
    smem = pl.BlockSpec(memory_space=pltpu.SMEM)
    vmem = pl.BlockSpec(memory_space=pltpu.VMEM)
    hbm = pl.BlockSpec(memory_space=pl.ANY)
    dma = pltpu.SemaphoreType.DMA
    block = (planes, rows, cols)
    others = max(groups - 1, 1)
    out = pl.pallas_call(
        functools.partial(kernel, dims),
        out_shape=(
            jax.ShapeDtypeStruct(forward_pair.shape, F32),
            jax.ShapeDtypeStruct(adjoint_pair.shape, F32),
            jax.ShapeDtypeStruct(momentum.shape, F32),
            jax.ShapeDtypeStruct(momentum.shape, F32),
        ),
        in_specs=[smem, smem, smem, vmem, vmem] + [hbm] * 6,
        out_specs=(hbm,) * 4,
        scratch_shapes=[
            pltpu.VMEM((2, 2, planes + 8, rows + 16, cols), F32),
            pltpu.VMEM((planes + 8, rows + 16, cols), F32),
            pltpu.VMEM(block, F32),
            pltpu.VMEM((steps + 2,) + block, BF),
            pltpu.VMEM((q, rows, cols), F32),
            pltpu.VMEM((4,) + block, F32),
            pltpu.VMEM((steps,) + block, F32),
            pltpu.VMEM((4 * rows, 2 * cols), F32),
            pltpu.VMEM(block, F32),
            pltpu.VMEM((others, q, rows, cols), F32),
            pltpu.VMEM((q, rows, cols), F32),
            pltpu.VMEM((q, rows, cols), F32),
            pltpu.VMEM((3 * cols, 2 * cols), BF),
            dma((steps, 2, 2)), dma((steps, 2, 2)),
            dma((steps, 2, 3, 2)), dma((steps, 2, 3, 2)),
            dma((2, 2)), dma((2, 2)),
            dma((others,)), dma((others,)),
            dma((8,)), dma((6,)),
        ],
        compiler_params=pltpu.CompilerParams(collective_id=0, has_side_effects=True),
    )(
        assignment, source_cells, wavelet, receiver_cells, residuals,
        model_field, buoyancy, forward_pair, adjoint_pair, stored_states, momentum,
    )
    return tuple(out)


def solution(mesh):
    in_specs = (
        P(("inv", "depth"), "lat", None),
        P(("inv", "depth"), "lat", None),
        P(("inv", "shot"), None, "depth", "lat", None),
        P(("inv", "shot"), None, "depth", "lat", None),
        P(("inv", "shot"), None, "depth", "lat", None),
        P(("inv", "depth", "shot"), "lat", None),
        P("inv", None),
        P("inv", None, None),
        P("inv"),
        P("inv", None),
        P("inv"),
    )
    out_specs = (
        P(("inv", "shot"), None, "depth", "lat", None),
        P(("inv", "shot"), None, "depth", "lat", None),
        P(("inv", "depth", "shot"), "lat", None),
        P(("inv", "depth", "shot"), "lat", None),
    )
    return jax.shard_map(local, mesh=mesh, in_specs=in_specs, out_specs=out_specs, check_vma=False)
```

time: 239 us -> 31.5 us (0.13)
  other arithmetic: 114 us -> 0 us
  starting transfers between devices: 48.5 us -> 0 us
  between operations: 31.8 us -> 0.66 us
  Pallas kernels: 0 us -> 26 us
  local copies, waits for them, and re-layouts: 25.5 us -> 4.56 us
  waiting for transfers between devices: 18.1 us -> 0 us
    scatter-add x4 -> x0, other arithmetic: 61 us -> none  [place_values(): field.at[depth_safe, row_safe, column_index]]
    ppermute x20 -> x0, starting transfers between devices: 48.4 us -> none  [the longest x10 35.2 us: extended(): lax.ppermute(tail, axis, [(i, (i + 1) % count) for i in range(ends)])]
    pallas_call x0 -> x1, Pallas kernels: none -> 26 us  [local(): pl.pallas_call(functools.partial(kernel, dims), out_shape=(jax.ShapeDtype...]
    another operation x37 -> x0, other arithmetic: 23.1 us -> none  [the longest x27 12.6 us: local(): current = jnp.stack([fwd_next, adj_next])]
    ppermute x20 -> x0, waiting for transfers between devices: 18.1 us -> none  [the longest x10 12.7 us: extended(): lax.ppermute(head, axis, [((i + 1) % count, i) for i in range(ends)])]
    add x7 -> x0, other arithmetic: 16.1 us -> none  [the longest x4 13 us: local(): 2.0 * trim(current_ext, 4) - prev_core]
    slice x12 -> x0, local copies, waits for them, and re-layouts: 9.37 us -> none  [the longest x8 6.32 us: offset_core(): rolled = jnp.roll(core, -offset, axis=core.ndim - 1)]
    unnamed x116 -> x10, local copies, waits for them, and re-layouts: 9.6 us -> 4.56 us
  transfers between devices with their start and end apart: 21 -> 0, of which waited for: 11 -> 0; matrix products, arithmetic and copies ran while one was open for 25% -> 0% of each run, Pallas kernels for 0% -> 0%
where the time goes in v1:
time: 31.5 us; the launch traced here: 31.2 us
  Pallas kernels  26 us (83%)
  local copies, waits for them, and re-layouts  4.56 us (14%)
  between operations  0.66 us (2%)
    pallas_call x1, Pallas kernels, local(): pl.pallas_call(functools.partial(kernel, dims), out_shape=(jax.ShapeDtype...  26 us
    unnamed x10, local copies, waits for them, and re-layouts  4.56 us

profile of v1, /device:TPU:0, one launch (start us, length us, event | category | flops | bytes accessed | tf_op | source)
XLA Modules:
  0.0 31.2 jit_solution(15201115898285527879)
XLA Ops:
  0.6 26.0 %shard_map.138 = (f32[1,2,16,32,128]{4,3,2,1,0:T(8,128)}, f32[1,2,16,32,128]{4,3,2,1,0:T(8,128)}, f32[8,32,128]{2,1,0:T(8,128)}, f32[8,32,128]{2,1,0:T(8,128)}) custom-call(s32[4]{0:T(128)} %assign_ref.1, s32[4]{0:T(128)} %source_ref.1, f32[4,4]{1,0:T(4,128)} %wave_ref.1, s32[4,256]{1,0:T(4,128)} %recv_ref.1, f32[4,4,256]{2,1,0:T(4,128)} %resid_ref.1, ...), custom_call_target="tpu_custom_call" | custom-call | tf_op jit(solution)/shard_map/pallas_call | solution.py:397
  26.7 0.0 copy-start
  26.7 1.9 %copy.19 = f32[1,2,16,32,128]{4,3,2,1,0:T(8,128)} copy(f32[1,2,16,32,128]{4,3,2,1,0:T(8,128)} %get-tuple-element.8) | data formatting | bytes 1048576
  28.6 0.0 copy-done
  28.6 0.0 copy-start.2
  28.6 0.8 %copy.20 = f32[1,2,16,32,128]{4,3,2,1,0:T(8,128)} copy(f32[1,2,16,32,128]{4,3,2,1,0:T(8,128)S(1)} %copy-done) | data formatting | bytes 1048576
  29.4 0.2 copy-done.2
  29.6 0.0 copy-start.1
  29.6 0.7 %copy.21 = f32[8,32,128]{2,1,0:T(8,128)} copy(f32[8,32,128]{2,1,0:T(8,128)S(1)} %copy-done.2) | data formatting | bytes 262144
  30.3 0.3 copy-done.1
  30.6 0.7 %copy.22 = f32[8,32,128]{2,1,0:T(8,128)} copy(f32[8,32,128]{2,1,0:T(8,128)S(1)} %copy-done.1) | data formatting | bytes 262144
Async XLA Ops:
  26.7 1.9 %copy-start = (f32[1,2,16,32,128]{4,3,2,1,0:T(8,128)S(1)}, f32[1,2,16,32,128]{4,3,2,1,0:T(8,128)}, u32[]{:S(2)}) copy-start(f32[1,2,16,32,128]{4,3,2,1,0:T(8,128)} %get-tuple-element.9) | copy-start | bytes 1572868
  28.6 1.0 %copy-start.2 = (f32[8,32,128]{2,1,0:T(8,128)S(1)}, f32[8,32,128]{2,1,0:T(8,128)}, u32[]{:S(2)}) copy-start(f32[8,32,128]{2,1,0:T(8,128)} %get-tuple-element.10) | copy-start | bytes 393220
  29.6 1.0 %copy-start.1 = (f32[8,32,128]{2,1,0:T(8,128)S(1)}, f32[8,32,128]{2,1,0:T(8,128)}, u32[]{:S(2)}) copy-start(f32[8,32,128]{2,1,0:T(8,128)} %get-tuple-element.11) | copy-start | bytes 393220

commit v2 on v1

--- a/solution.py
+++ b/solution.py
@@ -15,6 +15,8 @@
 BF = jnp.bfloat16
 F32 = jnp.float32
 FWD, ADJ = 0, 1
+VMEM_WINDOW = 61 * 1024 * 1024
+VMEM_OUT = 24 * 1024 * 1024
 
 
 def split_div(value, size):
@@ -30,8 +32,8 @@
     assign_ref, source_ref, wave_ref, recv_ref, resid_ref,
     model_ref, buoy_ref, fpair_ref, apair_ref, states_ref, mom_ref,
     fout_ref, aout_ref, momout_ref, modout_ref,
-    ext, bext, model_v, states_v, mom_v, coef, inj, xder, img, share, momnew, modnew, wmat,
-    zsend, zrecv, ysend, yrecv, bsend, brecv, ssend, srecv, load, store,
+    ext, bext, model_v, states_v, mom_v, coef, inj, xder, img, share, wmat,
+    zsend, zrecv, ysend, yrecv, bsend, brecv, ssend, srecv, load,
 ):
     groups, n_depth, n_lat, planes, rows, cols, steps, n_rec = dims
     rows_all = rows * n_lat
@@ -40,6 +42,7 @@
     l = lax.axis_index("lat")
     s = lax.axis_index("shot")
     pairs = (fpair_ref, apair_ref)
+    outs = (fout_ref, aout_ref)
     core_p = pl.ds(4, planes)
     core_r = pl.ds(8, rows)
     has = {
@@ -226,16 +229,24 @@
 
         lax.fori_loop(0, planes, body, 0)
 
-    def diffs(pick, want_second):
+    def diffs(pick, want_second=True):
         first = None
         second = None
+
+        def add(total, tap, value):
+            return tap * value if total is None else total + tap * value
+
         for reach in range(1, 5):
+            f_tap, s_tap = FIRST_TAPS[reach - 1], SECOND_TAPS[reach - 1]
             ahead, behind = pick(reach), pick(-reach)
-            term = FIRST_TAPS[reach - 1] * (ahead - behind)
-            first = term if first is None else first + term
-            if want_second:
-                term = SECOND_TAPS[reach - 1] * (ahead + behind)
-                second = term if second is None else second + term
+            if ahead is not None and behind is not None:
+                first = add(first, f_tap, ahead - behind)
+                if want_second:
+                    second = add(second, s_tap, ahead + behind)
+            elif ahead is not None or behind is not None:
+                only = behind if ahead is None else ahead
+                first = add(first, -f_tap if ahead is None else f_tap, only)
+                second = add(second, s_tap, only)
         return first, second
 
     def coefficients(p0):
@@ -250,29 +261,56 @@
             coef[2, p] = m * sy
             coef[3, p] = m * xs[i * rows : (i + 1) * rows, cols:]
 
-    def advance(k, f, p0):
+    def target(k, f, p):
+        if k == steps - 1:
+            return outs[f].at[0, 1, p]
+        return ext.at[(k + 1) % 2, f, p + 4, core_r]
+
+    def x_all(k, f):
+        xder[f] = x_part(ext[k % 2, f, core_p, core_r])
+
+    def advance(k, f, p0, side=None):
         now, then = k % 2, (k + 1) % 2
-        xder[...] = x_part(ext[now, f, pl.ds(p0 + 4, 4), core_r])
         for i in range(4):
             p = p0 + i
-            fz, gz = diffs(lambda o: ext[now, f, p + 4 + o, core_r], True)
-            fy, gy = diffs(lambda o: ext[now, f, p + 4, pl.ds(8 + o, rows)], True)
-            xrow = pl.ds(i * rows, rows)
-            second = gz + gy + xder[xrow, pl.ds(0, cols)]
+
+            def z_pick(o):
+                if side == 0 and i + o < 0 or side == 1 and i + o > 3:
+                    return None
+                return ext[now, f, p + 4 + o, core_r]
+
+            fz, gz = diffs(z_pick)
+            fy, gy = diffs(lambda o: ext[now, f, p + 4, pl.ds(8 + o, rows)])
+            xrow = pl.ds(p * rows, rows)
             value = (
                 2.0 * ext[now, f, p + 4, core_r]
                 - ext[then, f, p + 4, core_r]
-                + coef[0, p] * second
+                + coef[0, p] * (gz + gy + xder[f, xrow, pl.ds(0, cols)])
                 + coef[1, p] * fz
                 + coef[2, p] * fy
-                + coef[3, p] * xder[xrow, pl.ds(cols, cols)]
+                + coef[3, p] * xder[f, xrow, pl.ds(cols, cols)]
             )
             if f == ADJ:
                 value = value + inj[k, p]
             else:
                 here = jnp.where(sdepth == p, scell, -1)
                 value = value + jnp.where(cell_ids == here, wave_ref[fshot, k], 0.0)
-            ext[then, f, p + 4, core_r] = value
+            target(k, f, p)[...] = value
+
+    def add_halo(k, f, side):
+        now = k % 2
+        p0 = chunks[side][0]
+        for i in range(4):
+            p = p0 + i
+
+            def z_pick(o):
+                if side == 0 and i + o < 0 or side == 1 and i + o > 3:
+                    return ext[now, f, p + 4 + o, core_r]
+                return None
+
+            fz, gz = diffs(z_pick)
+            place = target(k, f, p)
+            place[...] = place[...] + (coef[0, p] * gz + coef[1, p] * fz)
 
     loads["states"].wait()
     loads[("cur", ADJ)].wait()
@@ -281,19 +319,19 @@
     loads["buoy"].wait()
     for way in (0, 1):
         wait_recv(bcopy("lat", way), "lat", way)
-        wait_recv(bcopy("depth", way), "depth", way)
 
     def coef_body(c, carry):
         coefficients(c * 4)
         return carry
 
-    lax.fori_loop(0, planes // 4, coef_body, 0)
+    lax.fori_loop(1, planes // 4 - 1, coef_body, 0)
+    for way in (0, 1):
+        wait_recv(bcopy("depth", way), "depth", way)
+    coefficients(0)
+    coefficients(planes - 4)
     loads[("prev", ADJ)].wait()
     loads[("cur", FWD)].wait()
     loads[("prev", FWD)].wait()
-
-    outs = (fout_ref, aout_ref)
-    finals = []
 
     def share_copy(o):
         dest = lax.rem(s + o, groups)
@@ -303,11 +341,6 @@
             device_id={"shot": dest}, device_id_type=MESH,
         )
 
-    def finish(src, dst):
-        copy = pltpu.make_async_copy(src, dst, store.at[len(finals)])
-        copy.start()
-        finals.append(copy)
-
     for k in range(steps):
         last = k == steps - 1
         if k > 0:
@@ -315,9 +348,8 @@
         if last:
             for o in range(1, groups):
                 share_copy(o).start()
-            for f in (ADJ, FWD):
-                finish(ext.at[k % 2, f, core_p, core_r], outs[f].at[0, 0])
         for f in (ADJ, FWD):
+            x_all(k, f)
             if k >= 2:
                 for way in (0, 1):
                     wait_send(zcopy(k - 1, f, way), "depth", way)
@@ -326,8 +358,11 @@
             for c in (0, 1):
                 for way in (0, 1):
                     wait_recv(ycopy(k, f, c, way), "lat", way)
+                advance(k, f, chunks[c][0], c)
+        for f in (ADJ, FWD):
+            for c in (0, 1):
                 wait_recv(zcopy(k, f, 1 - c), "depth", 1 - c)
-                advance(k, f, chunks[c][0])
+                add_halo(k, f, c)
                 if not last:
                     start(zcopy(k + 1, f, c), "depth", c)
                     for way in (0, 1):
@@ -346,7 +381,7 @@
                     for way in (0, 1):
                         start(ycopy(k + 1, f, 2, way), "lat", way)
             if last:
-                finish(ext.at[(k + 1) % 2, f, core_p, core_r], outs[f].at[0, 1])
+                outs[f][0, 0] = ext[k % 2, f, core_p, core_r]
 
     loads["mom"].wait()
     for o in range(1, groups):
@@ -357,10 +392,8 @@
         for o in range(1, groups):
             gradient = gradient + share[o - 1, p]
         moment = MOMENT_KEEP * mom_v[p] + factor * gradient
-        momnew[p] = moment
-        modnew[p] = model_v[s * q + p] - STEP_RATE * moment
-    finish(momnew, momout_ref)
-    finish(modnew, modout_ref)
+        momout_ref[p] = moment
+        modout_ref[p] = model_v[s * q + p] - STEP_RATE * moment
     for o in range(1, groups):
         share_copy(o).wait_send()
     for way in (0, 1):
@@ -372,7 +405,17 @@
                 wait_send(zcopy(e, f, way), "depth", way)
                 for c in range(len(chunks)):
                     wait_send(ycopy(e, f, c, way), "lat", way)
-    for copy in finals:
+
+
+def to_memory(*refs):
+    count = (len(refs) - 1) // 2
+    sems = refs[-1]
+    copies = [
+        pltpu.make_async_copy(refs[i], refs[count + i], sems.at[i]) for i in range(count)
+    ]
+    for copy in copies:
+        copy.start()
+    for copy in copies:
         copy.wait()
 
 
@@ -390,20 +433,16 @@
     dims = (groups, n_depth, n_lat, planes, rows, cols, steps, n_rec)
     smem = pl.BlockSpec(memory_space=pltpu.SMEM)
     vmem = pl.BlockSpec(memory_space=pltpu.VMEM)
-    hbm = pl.BlockSpec(memory_space=pl.ANY)
+    hbm = pl.BlockSpec(memory_space=pltpu.HBM)
     dma = pltpu.SemaphoreType.DMA
     block = (planes, rows, cols)
     others = max(groups - 1, 1)
+    out_dims = (forward_pair.shape, adjoint_pair.shape, momentum.shape, momentum.shape)
     out = pl.pallas_call(
         functools.partial(kernel, dims),
-        out_shape=(
-            jax.ShapeDtypeStruct(forward_pair.shape, F32),
-            jax.ShapeDtypeStruct(adjoint_pair.shape, F32),
-            jax.ShapeDtypeStruct(momentum.shape, F32),
-            jax.ShapeDtypeStruct(momentum.shape, F32),
-        ),
+        out_shape=tuple(pltpu.VMEM(shape, F32) for shape in out_dims),
         in_specs=[smem, smem, smem, vmem, vmem] + [hbm] * 6,
-        out_specs=(hbm,) * 4,
+        out_specs=(vmem,) * 4,
         scratch_shapes=[
             pltpu.VMEM((2, 2, planes + 8, rows + 16, cols), F32),
             pltpu.VMEM((planes + 8, rows + 16, cols), F32),
@@ -412,24 +451,31 @@
             pltpu.VMEM((q, rows, cols), F32),
             pltpu.VMEM((4,) + block, F32),
             pltpu.VMEM((steps,) + block, F32),
-            pltpu.VMEM((4 * rows, 2 * cols), F32),
+            pltpu.VMEM((2, planes * rows, 2 * cols), F32),
             pltpu.VMEM(block, F32),
             pltpu.VMEM((others, q, rows, cols), F32),
-            pltpu.VMEM((q, rows, cols), F32),
-            pltpu.VMEM((q, rows, cols), F32),
             pltpu.VMEM((3 * cols, 2 * cols), BF),
             dma((steps, 2, 2)), dma((steps, 2, 2)),
             dma((steps, 2, 3, 2)), dma((steps, 2, 3, 2)),
             dma((2, 2)), dma((2, 2)),
             dma((others,)), dma((others,)),
-            dma((8,)), dma((6,)),
+            dma((8,)),
         ],
-        compiler_params=pltpu.CompilerParams(collective_id=0, has_side_effects=True),
+        compiler_params=pltpu.CompilerParams(
+            collective_id=0, has_side_effects=True, vmem_limit_bytes=VMEM_WINDOW
+        ),
     )(
         assignment, source_cells, wavelet, receiver_cells, residuals,
         model_field, buoyancy, forward_pair, adjoint_pair, stored_states, momentum,
     )
-    return tuple(out)
+    return pl.pallas_call(
+        to_memory,
+        out_shape=tuple(jax.ShapeDtypeStruct(shape, F32) for shape in out_dims),
+        in_specs=[vmem] * 4,
+        out_specs=(hbm,) * 4,
+        scratch_shapes=[dma((4,))],
+        compiler_params=pltpu.CompilerParams(vmem_limit_bytes=VMEM_OUT),
+    )(*out)
 
 
 def solution(mesh):

time: 31.5 us -> 26.1 us (0.83)
  local copies, waits for them, and re-layouts: 4.56 us -> 0 us
  Pallas kernels: 26 us -> 25.2 us
    unnamed x10 -> x0, local copies, waits for them, and re-layouts: 4.56 us -> none
    pallas_call x1 -> x2, Pallas kernels: 26 us -> 25.2 us  [the longest x1 24.1 us: local(): pl.pallas_call(functools.partial(kernel, dims), out_shape=tuple((pltpu.VM...]
where the time goes in v2:
time: 26.1 us; the launch traced here: 25.9 us
  Pallas kernels  25.2 us (97%)
  between operations  0.64 us (2%)
    pallas_call x1, Pallas kernels, local(): pl.pallas_call(functools.partial(kernel, dims), out_shape=tuple((pltpu.VM...  24.1 us
    pallas_call x1, Pallas kernels, local(): pl.pallas_call(to_memory, out_shape=tuple((jax.ShapeDtypeStruct(shape, F3...  1.08 us

profile of v2, /device:TPU:0, one launch (start us, length us, event | category | flops | bytes accessed | tf_op | source)
XLA Modules:
  0.0 25.9 jit_solution(18335215092858093554)
XLA Ops:
  0.6 24.1 %shard_map.138 = (f32[1,2,16,32,128]{4,3,2,1,0:T(8,128)S(1)}, f32[1,2,16,32,128]{4,3,2,1,0:T(8,128)S(1)}, f32[8,32,128]{2,1,0:T(8,128)S(1)}, f32[8,32,128]{2,1,0:T(8,128)S(1)}) custom-call(s32[4]{0:T(128)} %assign_ref.1, s32[4]{0:T(128)} %source_ref.1, f32[4,4]{1,0:T(4,128)} %wave_ref.1, s32[4,256]{1,0:T(4,128)} %recv_ref.1, f32[4,4,256]{2,1,0:T(4,128)} %resid_ref.1, ...), custom_call_target="tpu_custom_call" | custom-call | tf_op jit(solution)/shard_map/pallas_call | solution.py:441
  24.8 1.1 %shard_map.139 = (f32[1,2,16,32,128]{4,3,2,1,0:T(8,128)}, f32[1,2,16,32,128]{4,3,2,1,0:T(8,128)}, f32[8,32,128]{2,1,0:T(8,128)}, f32[8,32,128]{2,1,0:T(8,128)}) custom-call(f32[1,2,16,32,128]{4,3,2,1,0:T(8,128)S(1)} %get-tuple-element.8.refs_0_, f32[1,2,16,32,128]{4,3,2,1,0:T(8,128)S(1)} %get-tuple-element.9.refs_1_, ...), custom_call_target="tpu_custom_call" | custom-call | tf_op jit(solution)/shard_map/pallas_call | solution.py:471

commit v3 on v2

--- a/solution.py
+++ b/solution.py
@@ -67,17 +67,6 @@
     begin("states", states_ref.at[0], states_v)
     begin("mom", mom_ref, mom_v)
 
-    for lo in (0, planes + 4):
-        for slot in range(2):
-            for f in range(2):
-                ext[slot, f, pl.ds(lo, 4), core_r] = jnp.zeros((4, rows, cols), F32)
-        bext[pl.ds(lo, 4), core_r] = jnp.zeros((4, rows, cols), F32)
-    for lo in (0, rows + 8):
-        for slot in range(2):
-            for f in range(2):
-                ext[slot, f, core_p, pl.ds(lo, 8)] = jnp.zeros((planes, 8, cols), F32)
-        bext[core_p, pl.ds(lo, 8)] = jnp.zeros((planes, 8, cols), F32)
-
     barrier = pltpu.get_barrier_semaphore()
     total = groups - 1
     for (axis, way), there in has.items():
@@ -157,6 +146,24 @@
             start(zcopy(0, f, way), "depth", way)
             for c in range(len(chunks)):
                 start(ycopy(0, f, c, way), "lat", way)
+
+    for way, lo in ((0, 0), (1, planes + 4)):
+
+        @pl.when(jnp.logical_not(has[("depth", way)]))
+        def _(lo=lo):
+            for f in range(2):
+                for slot in range(2):
+                    ext[slot, f, pl.ds(lo, 4), core_r] = jnp.zeros((4, rows, cols), F32)
+            bext[pl.ds(lo, 4), core_r] = jnp.zeros((4, rows, cols), F32)
+
+    for way, lo in ((0, 0), (1, rows + 8)):
+
+        @pl.when(jnp.logical_not(has[("lat", way)]))
+        def _(lo=lo):
+            for f in range(2):
+                for slot in range(2):
+                    ext[slot, f, core_p, pl.ds(lo, 8)] = jnp.zeros((planes, 8, cols), F32)
+            bext[core_p, pl.ds(lo, 8)] = jnp.zeros((planes, 8, cols), F32)
 
     delta = lax.broadcasted_iota(jnp.int32, (cols, cols), 0) - lax.broadcasted_iota(
         jnp.int32, (cols, cols), 1
@@ -343,9 +350,9 @@
 
     for k in range(steps):
         last = k == steps - 1
-        if k > 0:
+        if 0 < k and (steps < 2 or not last):
             imaging(k)
-        if last:
+        if last and steps < 2:
             for o in range(1, groups):
                 share_copy(o).start()
         for f in (ADJ, FWD):
@@ -367,7 +374,6 @@
                     start(zcopy(k + 1, f, c), "depth", c)
                     for way in (0, 1):
                         start(ycopy(k + 1, f, c, way), "lat", way)
-        for f in (ADJ, FWD):
             if len(chunks) > 2:
                 for way in (0, 1):
                     wait_recv(ycopy(k, f, 2, way), "lat", way)
@@ -380,6 +386,10 @@
                 if not last:
                     for way in (0, 1):
                         start(ycopy(k + 1, f, 2, way), "lat", way)
+            if f == ADJ and k == steps - 2:
+                imaging(steps - 1)
+                for o in range(1, groups):
+                    share_copy(o).start()
             if last:
                 outs[f][0, 0] = ext[k % 2, f, core_p, core_r]
 

time: 26.1 us -> 25.1 us (0.962)
  Pallas kernels: 25.2 us -> 24.2 us
    pallas_call x1, Pallas kernels: 24.1 us -> 23.1 us  [local(): pl.pallas_call(functools.partial(kernel, dims), out_shape=tuple((pltpu.VM...]
where the time goes in v3:
time: 25.1 us; the launch traced here: 24.8 us
  Pallas kernels  24.2 us (96%)
  between operations  0.64 us (3%)
    pallas_call x1, Pallas kernels, local(): pl.pallas_call(functools.partial(kernel, dims), out_shape=tuple((pltpu.VM...  23.1 us
    pallas_call x1, Pallas kernels, local(): pl.pallas_call(to_memory, out_shape=tuple((jax.ShapeDtypeStruct(shape, F3...  1.08 us

profile of v3, /device:TPU:0, one launch (start us, length us, event | category | flops | bytes accessed | tf_op | source)
XLA Modules:
  0.0 24.8 jit_solution(7567531021023939256)
XLA Ops:
  0.6 23.1 %shard_map.138 = (f32[1,2,16,32,128]{4,3,2,1,0:T(8,128)S(1)}, f32[1,2,16,32,128]{4,3,2,1,0:T(8,128)S(1)}, f32[8,32,128]{2,1,0:T(8,128)S(1)}, f32[8,32,128]{2,1,0:T(8,128)S(1)}) custom-call(s32[4]{0:T(128)} %assign_ref.1, s32[4]{0:T(128)} %source_ref.1, f32[4,4]{1,0:T(4,128)} %wave_ref.1, s32[4,256]{1,0:T(4,128)} %recv_ref.1, f32[4,4,256]{2,1,0:T(4,128)} %resid_ref.1, ...), custom_call_target="tpu_custom_call" | custom-call | tf_op jit(solution)/shard_map/pallas_call | solution.py:451
  23.7 1.1 %shard_map.139 = (f32[1,2,16,32,128]{4,3,2,1,0:T(8,128)}, f32[1,2,16,32,128]{4,3,2,1,0:T(8,128)}, f32[8,32,128]{2,1,0:T(8,128)}, f32[8,32,128]{2,1,0:T(8,128)}) custom-call(f32[1,2,16,32,128]{4,3,2,1,0:T(8,128)S(1)} %get-tuple-element.8.refs_0_, f32[1,2,16,32,128]{4,3,2,1,0:T(8,128)S(1)} %get-tuple-element.9.refs_1_, ...), custom_call_target="tpu_custom_call" | custom-call | tf_op jit(solution)/shard_map/pallas_call | solution.py:481
